TPU v7x, 32 devices: a whole 2x2x4 slice. The times are simulated.
32 devices in a mesh: pix: 4 (over z), mode: 8 (over y, x, core).
Axes of the slice: x: 2, y: 2, z: 4, core: 2. Of those that a mesh axis runs over, the one named last changes fastest.
Arguments:
- frames: float32 [4, 4096, 8192], P(None, 'pix', 'mode'), may hold values from 0 to 500, as said below
- phase_steps: int32 [4], replicated, may hold values from 0 to 3, each once
- pattern_rows: int32 [8192], replicated, may hold values from 0 to 8191, each once
- probes: float32 [2, 32, 8192], replicated, may hold values from -6 to 6
Outputs:
- channels: float32 [2, 32, 8192], replicated
- fields: float32 [2, 32, 4096], P(None, None, ('pix', 'mode'))
- strengths: float32 [32], replicated
Inputs may be any that keep to these rules, and one draw needn't show every extreme that they name: `phase_steps`: each frame has its own phase step. `pattern_rows`: every Hadamard row is displayed exactly once. `frames`: intensities are not negative.
All inputs are finite; a program needn't handle non-finite values.
Results may differ from a plain program's by a relative error of at most 0.0003.
Values sent between devices are 32-bit elements; how exact they have to be, the bound alone decides.
No kernel may reach another device: no remote copies, remote signals or barrier semaphores. Data moves between devices by JAX's collectives and lax.ppermute only.
A program may use at most 128 MiB of HBM per device.

v0:
```python
import math
import jax
import jax.numpy as jnp
from jax import lax
from jax.sharding import PartitionSpec as P

HB = 128
ITERS = 2
precise = lax.Precision.HIGHEST


def demodulate(frames, phase_steps):
    cosine = (phase_steps == 0).astype(jnp.float32) - (phase_steps == 2).astype(jnp.float32)
    sine_part = (phase_steps == 1).astype(jnp.float32) - (phase_steps == 3).astype(jnp.float32)
    real_part = cosine[0] * frames[0]
    imag_part = sine_part[0] * frames[0]
    for frame_index in range(1, frames.shape[0]):
        real_part = real_part + cosine[frame_index] * frames[frame_index]
        imag_part = imag_part + sine_part[frame_index] * frames[frame_index]
    return (0.25 * real_part, 0.25 * imag_part)


def sign_table(table_order):
    positions = jnp.arange(table_order, dtype=jnp.int32)
    common = positions[:, None] & positions[None, :]
    parity = jnp.zeros((table_order, table_order), jnp.int32)
    for bit_place in range(table_order.bit_length() - 1):
        parity = parity + (common >> bit_place & 1)
    return (1 - 2 * (parity & 1)).astype(jnp.float32)


def hadamard_rows(values):
    length = values.shape[-1]
    leading = values.shape[:-1]
    inner_signs = sign_table(HB)
    outer_signs = sign_table(length // HB)
    shaped = values.reshape((-1, length // HB, HB))
    shaped = jnp.matmul(shaped, inner_signs, precision=precise)
    shaped = jnp.einsum("ab,nbc->nac", outer_signs, shaped, precision=precise)
    return shaped.reshape(leading + (length,)) * (1.0 / math.sqrt(length))


def contract_last(first_arg, second_arg):
    return lax.dot_general(first_arg, second_arg, (((1,), (1,)), ((), ())), precision=precise)


def forward(matrix, vectors):
    real_out = contract_last(vectors[0], matrix[0]) - contract_last(vectors[1], matrix[1])
    imag_out = contract_last(vectors[1], matrix[0]) + contract_last(vectors[0], matrix[1])
    return jnp.stack([real_out, imag_out])


def backward(matrix, images):
    real_out = jnp.dot(images[0], matrix[0], precision=precise) + jnp.dot(
        images[1], matrix[1], precision=precise
    )
    imag_out = jnp.dot(images[1], matrix[0], precision=precise) - jnp.dot(
        images[0], matrix[1], precision=precise
    )
    return jnp.stack([real_out, imag_out])


def orthonormal(vectors):
    mode_count = vectors.shape[2]
    stacked = jnp.concatenate([vectors[0], vectors[1]], axis=1)
    gram_matrix = jnp.dot(stacked, stacked.T, precision=precise)
    factor = jnp.linalg.cholesky(gram_matrix)
    solved = lax.linalg.triangular_solve(factor, stacked, left_side=True, lower=True)
    return jnp.stack([solved[:, :mode_count], solved[:, mode_count:]])


def local(frames, phase_steps, pattern_rows, probes):
    columns = frames.shape[2]
    groups = lax.axis_size("mode")
    modes_total = columns * groups
    devices = lax.axis_size("pix") * groups
    real_part, imag_part = demodulate(frames, phase_steps)
    positions = jnp.arange(modes_total, dtype=jnp.int32)
    inverse = jnp.zeros((modes_total,), jnp.int32).at[pattern_rows].set(positions)
    current = orthonormal(probes)
    rows_here = real_part.shape[0] // groups
    demodulated = jnp.stack([real_part, imag_part]).reshape(2, groups, rows_here, columns)
    ordered = jnp.take(
        lax.all_to_all(demodulated, "mode", split_axis=1, concat_axis=3, tiled=True),
        inverse,
        axis=3,
    )
    matrix = hadamard_rows(ordered)
    matrix = matrix.reshape(2, rows_here, modes_total)
    for iteration in range(ITERS):
        images = forward(matrix, current)
        returned = lax.psum(backward(matrix, images), ("pix", "mode"))
        current = orthonormal(returned)
    fields = forward(matrix, current)
    local_power = jnp.sum(fields * fields, axis=(0, 2))
    strengths = lax.psum(local_power, ("pix", "mode")) / (fields.shape[2] * devices)
    channels = math.sqrt(modes_total) * current
    return (channels, fields, strengths)


def solution(mesh):
    in_specs = (P(None, "pix", "mode"), P(), P(), P())
    out_specs = (P(), P(None, None, ("pix", "mode")), P())
    return jax.shard_map(local, mesh=mesh, in_specs=in_specs, out_specs=out_specs, check_vma=False)
```

profile of v0, /device:TPU:0, one launch (start us, length us, event | category | flops | bytes accessed | tf_op | source)
XLA Modules:
  0.0 704.6 jit_solution(8088165573559418275)
XLA Ops:
  8.5 12.0 %add_multiply_fusion.1 = (f32[1,1024,1024]{2,1,0:T(8,128)S(1)}, f32[1,1024,1024]{2,1,0:T(8,128)S(1)}) fusion(f32[4,1024,1024]{2,1,0:T(8,128)} %param.7, f32[]{:T(128)} %bitcast.9, f32[]{:T(128)} %bitcast.8, f32[]{:T(128)} %bitcast.7, f32[]{:T(128)} %bitcast.6, f32[]{:T(128)} %bitcast.14, f32[]{:T(128)} %bitcast.13, f32[]{:T(128)} %bitcast.12, f32[]{:T(128)} %bitcast.11), kind=kLoop, calls=%fused_computation.52 | loop fusion | flops 16777216 | bytes 25165856 | tf_op jit(solution)/shard_map/mul | solution.py:20
  26.3 5.3 all-to-all-start
  41.4 30.7 %scatter_custom_fusion = s32[8192]{0:T(1024)S(1)} fusion(s32[8192]{0:T(1024)S(1)} %compare_select_fusion.1, s32[8192]{0:T(1024)S(1)} %iota.46, s32[]{:T(128)} %constant.66.clone.1), kind=kCustom, calls=%fused_computation.208 | custom fusion | bytes 32772 | tf_op jit(solution)/shard_map/scatter | solution.py:79
  75.2 50.9 %all-to-all-done = f32[2,8,128,1024]{3,2,0,1:T(8,128)} async-done(((f32[2,8,128,1024]{3,2,0,1:T(8,128)}), f32[2,8,128,1024]{3,2,0,1:T(8,128)}, u32[]{:S(2)}, u32[]{:S(2)}) %all-to-all-start) | async-done | bytes 8388640 | tf_op jit(solution)/shard_map/all_to_all | solution.py:84
  126.1 8.7 %copy.22 = f32[2,8,128,1024]{2,3,1,0:T(8,128)} copy(f32[2,8,128,1024]{3,2,0,1:T(8,128)} %all-to-all-done) | data formatting | bytes 16777216 | tf_op jit(solution)/shard_map/all_to_all | solution.py:84
  134.8 15.4 %copy.23 = f32[2,128,8192]{1,0,2:T(2,128)} copy(f32[2,128,8192]{1,2,0:T(8,128)} %bitcast.173) | data formatting | bytes 16777216 | tf_op jit(solution)/shard_map/all_to_all | solution.py:84
  150.1 59.4 %gather_fusion = f32[8192,2,128]{2,1,0:T(2,128)} fusion(f32[2,128,8192]{1,0,2:T(2,128)} %copy.23, s32[8192]{0:T(1024)S(1)} %fusion.166), kind=kCustom, calls=%fused_computation | custom fusion | bytes 16809984 | tf_op jit(solution)/shard_map/jit(_take)/gather | solution.py:83
  209.5 11.5 %gather.7 = f32[256,64,128]{0,2,1:T(8,128)} reshape(f32[2,128,8192]{1,0,2:T(2,128)} %bitcast.172) | data formatting | bytes 16777216 | tf_op jit(solution)/shard_map/jit(_take)/gather | solution.py:83
  221.0 8.7 %copy.24 = f32[256,64,128]{2,1,0:T(8,128)} copy(f32[256,64,128]{0,2,1:T(8,128)} %gather.7) | data formatting | bytes 16777216 | tf_op jit(solution)/shard_map/jit(_take)/gather | solution.py:83
  229.7 13.0 %fusion.4 = f32[256,64,128]{2,1,0:T(8,128)S(1)} fusion(f32[256,64,128]{2,1,0:T(8,128)} %copy.24, pred[64,128]{1,0:T(8,128)(4,1)S(1)} %and_bitcast_fusion), kind=kOutput, calls=%fused_computation.12 | convolution fusion | flops 3223732224 | bytes 16785408 | tf_op jit(solution)/shard_map/dot_general | solution.py:38
  242.8 8.9 %multiply_bitcast_fusion = f32[256,64,128]{2,1,0:T(8,128)S(1)} fusion(f32[256,64,128]{2,1,0:T(8,128)S(1)} %fusion.4), kind=kOutput, calls=%fused_computation.11 | convolution fusion | flops 1612800000 | bytes 16777216 | tf_op jit(solution)/shard_map/ab,nbc->nac/dot_general | solution.py:39
  253.3 5.8 fusion.20
  259.1 5.6 fusion.18
  264.7 5.6 fusion.70
  270.3 4.8 fusion.38
  275.0 5.7 fusion.73
  280.7 4.9 fusion.34
  285.6 4.6 fusion.3
  290.2 4.6 fusion.2
  296.6 134.8 %all-reduce.3.cloned.1.call-done = f32[2,32,8192]{2,1,0:T(8,128)} async-done(((f32[2,32,8192]{2,1,0:T(8,128)}), f32[2,32,8192]{2,1,0:T(8,128)}) %all-reduce.3.cloned.1.call-update) | async-done | bytes 2097168 | tf_op jit(solution)/shard_map/psum | solution.py:92
  443.9 5.6 fusion.14
  449.4 5.8 fusion.12
  455.2 5.6 fusion.76
  465.3 6.0 fusion.79
  475.9 4.8 fusion.1
  480.7 4.6 fusion
  486.8 133.5 %all-reduce.5.cloned.1.call-done = f32[2,32,8192]{2,1,0:T(8,128)} async-done(((f32[2,32,8192]{2,1,0:T(8,128)}), f32[2,32,8192]{2,1,0:T(8,128)}) %all-reduce.5.cloned.1.call-update) | async-done | bytes 2097168 | tf_op jit(solution)/shard_map/psum | solution.py:92
  632.7 5.8 fusion.8
  638.5 5.6 fusion.6
  644.3 5.8 fusion.85
  650.1 5.6 fusion.91
  656.4 38.9 %psum.23 = f32[32]{0:T(128)S(1)} all-reduce(f32[32]{0:T(128)S(1)} %get-tuple-element.5), channel_id=1, replica_groups=mesh['pix'=4,'mode'=8] {'pix','mode'}, use_global_device_ids=true, to_apply=%region_6.9 | all-reduce | flops 32 | bytes 256 | tf_op jit(solution)/shard_map/psum | solution.py:96
  (69 shorter events, 61.6 us)
Async XLA Ops:
  26.3 5.4 copy-start.7
  26.3 99.8 %all-to-all-start = ((f32[2,8,128,1024]{3,2,0,1:T(8,128)}), f32[2,8,128,1024]{3,2,0,1:T(8,128)}, u32[]{:S(2)}, u32[]{:S(2)}) async-start(f32[2,8,128,1024]{3,2,0,1:T(8,128)} %copy.21), calls=%async_computation | async-start | bytes 16777216 | tf_op jit(solution)/shard_map/all_to_all | solution.py:84
  31.6 9.7 %copy-start.8 = (s32[8192]{0:T(1024)S(1)}, s32[8192]{0:T(1024)}, u32[]{:S(2)}) copy-start(s32[8192]{0:T(1024)} %param.9) | copy-start | bytes 98308
  31.6 399.8 %all-reduce.3.cloned.1.call-start = ((), (), s32[]{:S(2)}) async-start(), calls=%async_computation.1 | async-start | bytes 4194304 | tf_op jit(solution)/shard_map/psum | solution.py:92
  31.8 1.0 copy-start.6
  253.3 27.4 %copy-start = (f32[128,64,128]{2,1,0:T(8,128)}, f32[128,64,128]{2,1,0:T(8,128)S(1)}, u32[]{:S(2)}) copy-start(f32[128,64,128]{2,1,0:T(8,128)S(1)} %get-tuple-element.9) | copy-start | bytes 12582916
  253.3 36.9 %copy-start.3 = (f32[128,64,128]{2,1,0:T(8,128)}, f32[128,64,128]{2,1,0:T(8,128)S(1)}, u32[]{:S(2)}) copy-start(f32[128,64,128]{2,1,0:T(8,128)S(1)} %get-tuple-element.10) | copy-start | bytes 12582916
  296.4 323.9 %all-reduce.5.cloned.1.call-start = ((), (), s32[]{:S(2)}) async-start(), calls=%async_computation.2 | async-start | bytes 4194304 | tf_op jit(solution)/shard_map/psum | solution.py:92
  441.6 2.2 copy-start.4
  443.9 11.4 %copy-start.1 = (f32[128,64,128]{2,1,0:T(8,128)S(1)}, f32[128,64,128]{2,1,0:T(8,128)}, u32[]{:S(2)}) copy-start(f32[128,64,128]{2,1,0:T(8,128)} %copy-done) | copy-start | bytes 12582916
  630.5 2.2 copy-start.5
  638.5 5.7 copy-start.2
Sparse Core Ops, SparseCore 0:
  296.5 134.8 all-reduce.2
  486.9 133.3 all-reduce.4
where the time goes:
time: 711 us; the launch traced here: 705 us
  waiting for transfers between devices  319 us (45%)
  local copies, waits for them, and re-layouts  146 us (21%)
  matrix products  140 us (20%)
  other arithmetic  40.2 us (6%)
  blocking collectives  38.9 us (5%)
  between operations  14.9 us (2%)
    psum x2, waiting for transfers between devices, local(): returned = lax.psum(backward(matrix, images), ('pix', 'mode'))  268 us
    gather x3, local copies, waits for them, and re-layouts, local(): jnp.take(lax.all_to_all(demodulated, 'mode', split_axis=1, concat_axis=3,...  79.6 us
    dot_general x12, matrix products, contract_last(): lax.dot_general(first_arg, second_arg, (((1,), (1,)), ((), ())), precisio...  68.3 us
    all_to_all x1, waiting for transfers between devices, local(): lax.all_to_all(demodulated, 'mode', split_axis=1, concat_axis=3, tiled=True)  50.9 us
    psum x1, blocking collectives, local(): lax.psum(local_power, ('pix', 'mode')) / (fields.shape[2] * devices)  38.9 us
    scatter x1, local copies, waits for them, and re-layouts, local(): jnp.zeros((modes_total,), jnp.int32).at[pattern_rows].set(positions)  30.7 us
    all_to_all x2, local copies, waits for them, and re-layouts, local(): lax.all_to_all(demodulated, 'mode', split_axis=1, concat_axis=3, tiled=True)  24 us
  transfers between devices with their start and end apart: 3, of which 3 were waited for; matrix products, arithmetic and copies ran while one was open for 6% of the time, Pallas kernels for 0%

commit v1 on v0

--- a/solution.py
+++ b/solution.py
@@ -7,6 +7,27 @@
 HB = 128
 ITERS = 2
 precise = lax.Precision.HIGHEST
+
+
+def guide_heaps(inputs, dev_axis="mode"):
+    outcome_arr = lax.axis_size(dev_axis)
+    then, found_now = (outcome_arr, lax.axis_index(dev_axis))
+    prior = inputs.shape[1] // then
+    current_block = list(inputs.shape)
+    current_block[1] = prior
+    current_value = current_block[3]
+    current_block[3] = current_value * then
+    formed = jnp.zeros(current_block, inputs.dtype)
+    for nth in range(then):
+        q_next = lax.dynamic_slice_in_dim(inputs, (found_now ^ nth) * prior, prior, axis=1)
+        if nth:
+            q_next = lax.ppermute(
+                q_next, dev_axis, list(map(lambda i0: (i0, i0 ^ nth), range(then)))
+            )
+        formed = lax.dynamic_update_slice_in_dim(
+            formed, q_next, (found_now ^ nth) * current_value, axis=3
+        )
+    return formed
 
 
 def demodulate(frames, phase_steps):
@@ -80,11 +101,7 @@
     current = orthonormal(probes)
     rows_here = real_part.shape[0] // groups
     demodulated = jnp.stack([real_part, imag_part]).reshape(2, groups, rows_here, columns)
-    ordered = jnp.take(
-        lax.all_to_all(demodulated, "mode", split_axis=1, concat_axis=3, tiled=True),
-        inverse,
-        axis=3,
-    )
+    ordered = jnp.take(guide_heaps(demodulated), inverse, axis=3)
     matrix = hadamard_rows(ordered)
     matrix = matrix.reshape(2, rows_here, modes_total)
     for iteration in range(ITERS):

time: 711 us -> 727 us (1.023)
  waiting for transfers between devices: 319 us -> 303 us
  local copies, waits for them, and re-layouts: 146 us -> 160 us
  other arithmetic: 40.2 us -> 53.9 us
    all_to_all x1 -> x0, waiting for transfers between devices: 50.9 us -> none  [local(): lax.all_to_all(demodulated, 'mode', split_axis=1, concat_axis=3, tiled=True)]
    ppermute x0 -> x7, waiting for transfers between devices: none -> 33.2 us  [guide_heaps(): lax.ppermute(q_next, dev_axis, list(map(lambda i0: (i0, i0 ^ nth), range(...]
    all_to_all x2 -> x0, local copies, waits for them, and re-layouts: 24 us -> none  [local(): lax.all_to_all(demodulated, 'mode', split_axis=1, concat_axis=3, tiled=True)]
    dynamic_update_slice x0 -> x8, local copies, waits for them, and re-layouts: none -> 19 us  [guide_heaps(): lax.dynamic_update_slice_in_dim(formed, q_next, (found_now ^ nth) * curre...]
    another operation x1 -> x2, local copies, waits for them, and re-layouts: 4.06 us -> 21.8 us  [local(): jnp.stack([real_part, imag_part]).reshape(2, groups, rows_here, columns)]
    another operation x1 -> x2, other arithmetic: 1.65 us -> 11 us  [local(): jnp.stack([real_part, imag_part]).reshape(2, groups, rows_here, columns)]
    ppermute x0 -> x7, starting transfers between devices: none -> 7.69 us  [guide_heaps(): lax.ppermute(q_next, dev_axis, list(map(lambda i0: (i0, i0 ^ nth), range(...]
  transfers between devices with their start and end apart: 3 -> 9, of which waited for: 3 -> 4; matrix products, arithmetic and copies ran while one was open for 6% -> 9% of each run, Pallas kernels for 0% -> 0%
where the time goes in v1:
time: 727 us; the launch traced here: 718 us
  waiting for transfers between devices  303 us (42%)
  local copies, waits for them, and re-layouts  160 us (22%)
  matrix products  140 us (19%)
  other arithmetic  53.9 us (7%)
  blocking collectives  38.9 us (5%)
  between operations  15 us (2%)
  starting transfers between devices  7.95 us (1%)
    psum x2, waiting for transfers between devices, local(): returned = lax.psum(backward(matrix, images), ('pix', 'mode'))  270 us
    gather x3, local copies, waits for them, and re-layouts, local(): ordered = jnp.take(guide_heaps(demodulated), inverse, axis=3)  79.7 us
    dot_general x12, matrix products, contract_last(): lax.dot_general(first_arg, second_arg, (((1,), (1,)), ((), ())), precisio...  68.2 us
    psum x1, blocking collectives, local(): lax.psum(local_power, ('pix', 'mode')) / (fields.shape[2] * devices)  38.9 us
    ppermute x7, waiting for transfers between devices, guide_heaps(): lax.ppermute(q_next, dev_axis, list(map(lambda i0: (i0, i0 ^ nth), range(...  33.2 us
    scatter x1, local copies, waits for them, and re-layouts, local(): jnp.zeros((modes_total,), jnp.int32).at[pattern_rows].set(positions)  30.7 us
    another operation x2, local copies, waits for them, and re-layouts, local(): jnp.stack([real_part, imag_part]).reshape(2, groups, rows_here, columns)  21.8 us
    dynamic_update_slice x8, local copies, waits for them, and re-layouts, guide_heaps(): lax.dynamic_update_slice_in_dim(formed, q_next, (found_now ^ nth) * curre...  19 us
  transfers between devices with their start and end apart: 9, of which 4 were waited for; matrix products, arithmetic and copies ran while one was open for 9% of the time, Pallas kernels for 0%

profile of v1, /device:TPU:0, one launch (start us, length us, event | category | flops | bytes accessed | tf_op | source)
XLA Modules:
  0.0 718.0 jit_solution(3694104323222999715)
XLA Ops:
  8.6 14.5 %add_multiply_fusion.1 = (f32[1,1024,1024]{2,1,0:T(8,128)}, f32[1,1024,1024]{2,1,0:T(8,128)}) fusion(f32[4,1024,1024]{2,1,0:T(8,128)} %param.7, f32[]{:T(128)} %bitcast.9, f32[]{:T(128)} %bitcast.8, f32[]{:T(128)} %bitcast.7, f32[]{:T(128)} %bitcast.6, f32[]{:T(128)} %bitcast.14, f32[]{:T(128)} %bitcast.13, f32[]{:T(128)} %bitcast.12, f32[]{:T(128)} %bitcast.11), kind=kLoop, calls=%fused_computation.67 | loop fusion | flops 16777216 | bytes 25165856 | tf_op jit(solution)/shard_map/mul | solution.py:41
  23.1 10.9 %copy.15 = f32[1,8,128,1024]{2,0,3,1:T(1,128)} copy(f32[1,8,128,1024]{3,2,1,0:T(8,128)} %bitcast.185) | data formatting | bytes 8388608 | tf_op jit(solution)/shard_map/stack | solution.py:103
  33.9 10.9 %copy.14 = f32[1,8,128,1024]{2,0,3,1:T(1,128)} copy(f32[1,8,128,1024]{3,2,1,0:T(8,128)} %bitcast.184) | data formatting | bytes 8388608 | tf_op jit(solution)/shard_map/stack | solution.py:103
  44.9 9.0 %fusion.94 = (f32[2,1,128,1024]{2,0,3,1:T(2,128)}, f32[2,1,128,1024]{2,0,3,1:T(2,128)}, f32[2,1,128,1024]{2,0,3,1:T(2,128)}, f32[2,1,128,1024]{2,0,3,1:T(2,128)}...) fusion(s32[]{:T(128)S(6)} %select_n.82, f32[1,8,128,1024]{2,0,3,1:T(1,128)} %copy.14, ...), kind=kLoop, calls=%fused_computation.109 | loop fusion | flops 1572864 | bytes 14680088 | tf_op jit(solution)/shard_map/stack | solution.py:103
  66.1 5.4 broadcast.105
  78.8 30.7 %scatter_custom_fusion = s32[8192]{0:T(1024)S(1)} fusion(s32[8192]{0:T(1024)S(1)} %compare_select_fusion.1, s32[8192]{0:T(1024)S(1)} %iota.46, s32[]{:T(128)} %constant.35.clone.1), kind=kCustom, calls=%fused_computation.239 | custom fusion | bytes 32772 | tf_op jit(solution)/shard_map/scatter | solution.py:100
  127.0 12.8 %collective-permute-done.5 = f32[2,1,128,1024]{2,0,3,1:T(2,128)S(1)} collective-permute-done((f32[2,1,128,1024]{2,0,3,1:T(2,128)S(1)}, f32[2,1,128,1024]{2,0,3,1:T(2,128)S(1)}, u32[]{:S(2)}, u32[]{:S(2)}) %collective-permute-start.5) | collective-permute-done | bytes 1048608 | tf_op jit(solution)/shard_map/ppermute | solution.py:24
  140.8 20.4 %collective-permute-done.6 = f32[2,1,128,1024]{2,0,3,1:T(2,128)S(1)} collective-permute-done((f32[2,1,128,1024]{2,0,3,1:T(2,128)}, f32[2,1,128,1024]{2,0,3,1:T(2,128)S(1)}, u32[]{:S(2)}, u32[]{:S(2)}) %collective-permute-start.6) | collective-permute-done | bytes 1048608 | tf_op jit(solution)/shard_map/ppermute | solution.py:24
  162.3 59.4 %gather_fusion = f32[8192,2,128]{2,1,0:T(2,128)} fusion(f32[2,128,8192]{1,0,2:T(2,128)} %bitcast_dynamic-update-slice_fusion, s32[8192]{0:T(1024)S(1)} %fusion.174), kind=kCustom, calls=%fused_computation | custom fusion | bytes 16809984 | tf_op jit(solution)/shard_map/jit(_take)/gather | solution.py:104
  221.7 11.5 %gather.7 = f32[256,64,128]{0,2,1:T(8,128)} reshape(f32[2,128,8192]{1,0,2:T(2,128)} %bitcast.183) | data formatting | bytes 16777216 | tf_op jit(solution)/shard_map/jit(_take)/gather | solution.py:104
  233.2 8.7 %copy.16 = f32[256,64,128]{2,1,0:T(8,128)} copy(f32[256,64,128]{0,2,1:T(8,128)} %gather.7) | data formatting | bytes 16777216 | tf_op jit(solution)/shard_map/jit(_take)/gather | solution.py:104
  242.0 13.0 %fusion.4 = f32[256,64,128]{2,1,0:T(8,128)S(1)} fusion(f32[256,64,128]{2,1,0:T(8,128)} %copy.16, pred[64,128]{1,0:T(8,128)(4,1)S(1)} %and_bitcast_fusion), kind=kOutput, calls=%fused_computation.27 | convolution fusion | flops 3223732224 | bytes 16785408 | tf_op jit(solution)/shard_map/dot_general | solution.py:59
  255.0 8.9 %multiply_bitcast_fusion = f32[256,64,128]{2,1,0:T(8,128)S(1)} fusion(f32[256,64,128]{2,1,0:T(8,128)S(1)} %fusion.4), kind=kOutput, calls=%fused_computation.26 | convolution fusion | flops 1612800000 | bytes 16777216 | tf_op jit(solution)/shard_map/ab,nbc->nac/dot_general | solution.py:60
  265.5 5.8 fusion.18
  271.3 5.6 fusion.20
  276.9 5.6 fusion.73
  282.5 4.8 fusion.34
  287.3 5.6 fusion.70
  292.9 4.9 fusion.38
  308.8 136.1 %all-reduce.3.cloned.1.call-done = f32[2,32,8192]{2,1,0:T(8,128)} async-done(((f32[2,32,8192]{2,1,0:T(8,128)}), f32[2,32,8192]{2,1,0:T(8,128)}) %all-reduce.3.cloned.1.call-update) | async-done | bytes 2097168 | tf_op jit(solution)/shard_map/psum | solution.py:109
  457.4 5.6 fusion.12
  462.9 5.8 fusion.14
  468.7 5.6 fusion.79
  478.9 6.0 fusion.76
  489.4 4.8 fusion
  494.2 4.6 fusion.1
  500.3 133.6 %all-reduce.5.cloned.1.call-done = f32[2,32,8192]{2,1,0:T(8,128)} async-done(((f32[2,32,8192]{2,1,0:T(8,128)}), f32[2,32,8192]{2,1,0:T(8,128)}) %all-reduce.5.cloned.1.call-update) | async-done | bytes 2097168 | tf_op jit(solution)/shard_map/psum | solution.py:109
  646.3 5.8 fusion.6
  652.1 5.6 fusion.8
  657.6 5.9 fusion.91
  663.5 5.6 fusion.85
  669.8 38.9 %psum.23 = f32[32]{0:T(128)S(1)} all-reduce(f32[32]{0:T(128)S(1)} %get-tuple-element.5), channel_id=1, replica_groups=mesh['pix'=4,'mode'=8] {'pix','mode'}, use_global_device_ids=true, to_apply=%region_6.9 | all-reduce | flops 32 | bytes 256 | tf_op jit(solution)/shard_map/psum | solution.py:113
  (96 shorter events, 91.1 us)
Async XLA Ops:
  7.2 437.7 %all-reduce.3.cloned.1.call-start = ((), (), s32[]{:S(2)}) async-start(), calls=%async_computation | async-start | bytes 4194304 | tf_op jit(solution)/shard_map/psum | solution.py:109
  44.9 13.9 %copy-start.11 = (s32[8192]{0:T(1024)S(1)}, s32[8192]{0:T(1024)}, u32[]{:S(2)}) copy-start(s32[8192]{0:T(1024)} %param.9) | copy-start | bytes 98308
  44.9 13.9 %copy-start.9 = (f32[2,32,8192]{2,1,0:T(8,128)S(1)}, f32[2,32,8192]{2,1,0:T(8,128)}, u32[]{:S(2)}) copy-start(f32[2,32,8192]{2,1,0:T(8,128)} %param.10) | copy-start | bytes 6291460
  53.9 58.9 %collective-permute-start = (f32[2,1,128,1024]{2,0,3,1:T(2,128)}, f32[2,1,128,1024]{2,0,3,1:T(2,128)}, u32[]{:S(2)}, u32[]{:S(2)}) collective-permute-start(f32[2,1,128,1024]{2,0,3,1:T(2,128)} %get-tuple-element.12), channel_id=1, source_target_pairs={{0,1},{1,0},{2,3},{3,2},{4,5},{5,4},{6,7},{7,6},{8,9},{9,8},{10,11... | collective-permute-start | bytes 3145736 | tf_op jit(solution)/shard_map/ppermute | solution.py:24
  54.4 63.4 %collective-permute-start.1 = (f32[2,1,128,1024]{2,0,3,1:T(2,128)}, f32[2,1,128,1024]{2,0,3,1:T(2,128)}, u32[]{:S(2)}, u32[]{:S(2)}) collective-permute-start(f32[2,1,128,1024]{2,0,3,1:T(2,128)} %get-tuple-element.13), channel_id=1, source_target_pairs={{0,2},{1,3},{2,0},{3,1},{4,6},{5,7},{6,4},{7,5},{8,10},{9,11},{10,... | collective-permute-start | bytes 3145736 | tf_op jit(solution)/shard_map/ppermute | solution.py:24
  57.0 63.2 %collective-permute-start.2 = (f32[2,1,128,1024]{2,0,3,1:T(2,128)}, f32[2,1,128,1024]{2,0,3,1:T(2,128)}, u32[]{:S(2)}, u32[]{:S(2)}) collective-permute-start(f32[2,1,128,1024]{2,0,3,1:T(2,128)} %get-tuple-element.14), channel_id=1, source_target_pairs={{0,3},{1,2},{2,1},{3,0},{4,7},{5,6},{6,5},{7,4},{8,11},{9,10},{10,... | collective-permute-start | bytes 3145736 | tf_op jit(solution)/shard_map/ppermute | solution.py:24
  57.0 65.4 %collective-permute-start.3 = (f32[2,1,128,1024]{2,0,3,1:T(2,128)}, f32[2,1,128,1024]{2,0,3,1:T(2,128)}, u32[]{:S(2)}, u32[]{:S(2)}) collective-permute-start(f32[2,1,128,1024]{2,0,3,1:T(2,128)} %get-tuple-element.15), channel_id=1, source_target_pairs={{0,4},{1,5},{2,6},{3,7},{4,0},{5,1},{6,2},{7,3},{8,12},{9,13},{10,... | collective-permute-start | bytes 3145736 | tf_op jit(solution)/shard_map/ppermute | solution.py:24
  58.8 65.9 %collective-permute-start.4 = (f32[2,1,128,1024]{2,0,3,1:T(2,128)}, f32[2,1,128,1024]{2,0,3,1:T(2,128)}, u32[]{:S(2)}, u32[]{:S(2)}) collective-permute-start(f32[2,1,128,1024]{2,0,3,1:T(2,128)} %get-tuple-element.16), channel_id=1, source_target_pairs={{0,5},{1,4},{2,7},{3,6},{4,1},{5,0},{6,3},{7,2},{8,13},{9,12},{10,... | collective-permute-start | bytes 3145736 | tf_op jit(solution)/shard_map/ppermute | solution.py:24
  59.0 1.0 copy-start.8
  66.1 5.4 copy-start.6
  66.1 6.4 copy-start.7
  109.5 3.3 copy-start.10
  112.8 27.0 %collective-permute-start.5 = (f32[2,1,128,1024]{2,0,3,1:T(2,128)S(1)}, f32[2,1,128,1024]{2,0,3,1:T(2,128)S(1)}, u32[]{:S(2)}, u32[]{:S(2)}) collective-permute-start(f32[2,1,128,1024]{2,0,3,1:T(2,128)S(1)} %copy-done.10), channel_id=1, source_target_pairs={{0,6},{1,7},{2,4},{3,5},{4,2},{5,3},{6,0},{7,1},{8,14},{9,15},{10,... | collective-permute-start | bytes 3145736 | tf_op jit(solution)/shard_map/ppermute | solution.py:24
  117.8 43.4 %collective-permute-start.6 = (f32[2,1,128,1024]{2,0,3,1:T(2,128)}, f32[2,1,128,1024]{2,0,3,1:T(2,128)S(1)}, u32[]{:S(2)}, u32[]{:S(2)}) collective-permute-start(f32[2,1,128,1024]{2,0,3,1:T(2,128)} %get-tuple-element.11), channel_id=1, source_target_pairs={{0,7},{1,6},{2,5},{3,4},{4,3},{5,2},{6,1},{7,0},{8,15},{9,14},{10,... | collective-permute-start | bytes 3145736 | tf_op jit(solution)/shard_map/ppermute | solution.py:24
  265.5 27.4 %copy-start = (f32[128,64,128]{2,1,0:T(8,128)}, f32[128,64,128]{2,1,0:T(8,128)S(1)}, u32[]{:S(2)}) copy-start(f32[128,64,128]{2,1,0:T(8,128)S(1)} %get-tuple-element.9) | copy-start | bytes 12582916
  265.5 36.9 %copy-start.3 = (f32[128,64,128]{2,1,0:T(8,128)}, f32[128,64,128]{2,1,0:T(8,128)S(1)}, u32[]{:S(2)}) copy-start(f32[128,64,128]{2,1,0:T(8,128)S(1)} %get-tuple-element.10) | copy-start | bytes 12582916
  308.6 325.2 %all-reduce.5.cloned.1.call-start = ((), (), s32[]{:S(2)}) async-start(), calls=%async_computation.1 | async-start | bytes 4194304 | tf_op jit(solution)/shard_map/psum | solution.py:109
  455.1 2.2 copy-start.4
  457.4 11.4 %copy-start.1 = (f32[128,64,128]{2,1,0:T(8,128)S(1)}, f32[128,64,128]{2,1,0:T(8,128)}, u32[]{:S(2)}) copy-start(f32[128,64,128]{2,1,0:T(8,128)} %copy-done) | copy-start | bytes 12582916
  644.1 2.2 copy-start.5
  646.3 11.3 %copy-start.2 = (f32[128,64,128]{2,1,0:T(8,128)S(1)}, f32[128,64,128]{2,1,0:T(8,128)}, u32[]{:S(2)}) copy-start(f32[128,64,128]{2,1,0:T(8,128)} %copy-done) | copy-start | bytes 12582916
Sparse Core Ops, SparseCore 0:
  308.7 136.1 all-reduce.2
  500.4 133.3 all-reduce.4
